TPU v7x, 32 devices: a whole 2x2x4 slice. The times are simulated.
32 devices in a mesh: groups: 2 (over x), seq: 16 (over z, y, core).
Axes of the slice: x: 2, y: 2, z: 4, core: 2. Of those that a mesh axis runs over, the one named last changes fastest.
Arguments:
- queries: bfloat16 [4096, 5120], P(('groups', 'seq')), parts along dimension 0, may hold values from -12 to 12
- keys: bfloat16 [4096, 5120], P(('groups', 'seq')), parts along dimension 0, may hold values from -12 to 12
- values: bfloat16 [4096, 5120], P(('groups', 'seq')), parts along dimension 0, may hold values from -6 to 6
- q_gain: float32 [5120], replicated, may hold values from 0.1 to 1.9
- k_gain: float32 [5120], replicated, may hold values from 0.1 to 1.9
- key_tiles: int32 [40, 16, 16], replicated, may hold values from 0 to 15, as said below
- key_count: int32 [40, 16], replicated, may hold values from 1 to 16
Outputs:
- attended: bfloat16 [4096, 5120], P(('groups', 'seq')), parts along dimension 0
There are 2 independent parts, one for each index of `groups`. A program takes and returns all parts, laid end to end along the dimension named above; an argument that names none is the same for every part. Nothing has to cross between parts.
Inputs may be any that keep to these rules, and one draw needn't show every extreme that they name: key_tiles[h, t] holds 16 distinct tiles and its first entry is t itself.
All inputs are finite; a program needn't handle non-finite values.
Results may differ from a plain program's by a relative error of at most 0.012.
The roundings to bfloat16 on the way count: a program that leaves them out, or rounds other values in their place, can miss the bound.
Values may be sent and summed in bfloat16 or wider, within the bound.
A program may use at most 128 MiB of HBM per device.

v0:
```python
import functools
import math

import jax
import jax.numpy as jnp
from jax import lax
from jax.experimental import pallas as pl
from jax.experimental.pallas import tpu as pltpu
from jax.sharding import PartitionSpec as P

HEADS = 40
HEAD_DIM = 128
TILE = 128


group_size = 4


def normed(rows, gain):
    values32 = rows.astype(jnp.float32)
    factor = lax.rsqrt(jnp.mean(values32 * values32, axis=-1, keepdims=True) + 1e-06)
    return (values32 * factor * gain).astype(jnp.bfloat16)


def padded(entries, length):
    return jnp.pad(entries, (0, length - entries.shape[0]), mode="edge")


def attend_units(received, slot_index, tile_index, head_index, key_tiles, key_count):

    def one_group(unit_items):
        slot_part, tile_part, head_part = unit_items
        query_rows = received[tile_part, slot_part, 0]
        key_lists = key_tiles[head_part, tile_part]
        counts = key_count[head_part, tile_part]
        key_block = received[key_lists, slot_part[:, None], 1]
        value_block = received[key_lists, slot_part[:, None], 2]
        units = query_rows.shape[0]
        tile_rows = query_rows.shape[1]
        key_flat = key_block.reshape(units, -1, key_block.shape[-1])
        value_flat = value_block.reshape(units, -1, value_block.shape[-1])
        scores = jnp.einsum(
            "uqd,ukd->uqk", query_rows, key_flat, preferred_element_type=jnp.float32
        ) / math.sqrt(query_rows.shape[-1])
        list_place = jnp.arange(key_flat.shape[1]) // tile_rows
        valid = (list_place[None, :] < counts[:, None])[:, None, :]
        masked = jnp.where(valid, scores, -jnp.inf)
        peak = jnp.max(masked, axis=-1, keepdims=True)
        weights = jnp.where(valid, jnp.exp(masked - peak), jnp.float32(0.0))
        total = jnp.sum(weights, axis=-1, keepdims=True)
        probs = weights.astype(jnp.bfloat16)
        mixed = (
            jnp.einsum("uqk,ukd->uqd", probs, value_flat, preferred_element_type=jnp.float32)
            / total
        )
        return mixed.astype(jnp.bfloat16)

    grouped = (
        slot_index.reshape(-1, group_size),
        tile_index.reshape(-1, group_size),
        head_index.reshape(-1, group_size),
    )
    result = lax.map(one_group, grouped)
    return result.reshape(-1, result.shape[2], result.shape[3])


def exchanged(queries, keys, values, q_gain, k_gain, key_tiles, key_count):
    devices = lax.axis_size("seq")
    my_index = lax.axis_index("seq")
    q_normed = normed(queries, q_gain)
    k_normed = normed(keys, k_gain)
    stacked = (
        jnp.stack([q_normed, k_normed, values])
        .reshape(3, TILE, HEADS, HEAD_DIM)
        .transpose(2, 0, 1, 3)
    )
    targets = jnp.arange(devices)
    per_device = (HEADS + devices - 1) // devices
    total_slots = devices * per_device
    fewest_slots = total_slots // HEADS
    most_units = (devices + fewest_slots - 1) // fewest_slots

    def slot_layout(slot_number):
        head_of = slot_number * HEADS // total_slots
        head_start = (head_of * total_slots + HEADS - 1) // HEADS
        head_end = ((head_of + 1) * total_slots + HEADS - 1) // HEADS
        sharers = head_end - head_start
        within = slot_number - head_start
        return (head_of, within * devices // sharers, (within + 1) * devices // sharers)

    all_slots = jnp.arange(total_slots).reshape(devices, per_device)
    send_heads = slot_layout(all_slots)[0]
    received = lax.all_to_all(stacked[send_heads], "seq", split_axis=0, concat_axis=0, tiled=True)
    own_heads, lower_tile, upper_tile = slot_layout(my_index * per_device + jnp.arange(per_device))
    offsets = jnp.arange(most_units)
    tile_grid = jnp.minimum(lower_tile[:, None] + offsets[None, :], devices - 1)
    slot_grid = jnp.broadcast_to(jnp.arange(per_device)[:, None], tile_grid.shape)
    head_grid = jnp.broadcast_to(own_heads[:, None], tile_grid.shape)
    unit_total = per_device * most_units
    length = (unit_total + group_size - 1) // group_size * group_size
    finished = attend_units(
        received,
        padded(slot_grid.reshape(-1), length),
        padded(tile_grid.reshape(-1), length),
        padded(head_grid.reshape(-1), length),
        key_tiles,
        key_count,
    )[:unit_total]
    finished = finished.reshape(per_device, most_units, TILE, HEAD_DIM)
    position = targets[:, None] - lower_tile[None, :]
    inside = (position >= 0) & (targets[:, None] < upper_tile[None, :])
    gathered = finished[jnp.arange(per_device)[None, :], jnp.clip(position, 0, most_units - 1)]
    outgoing = jnp.where(inside[:, :, None, None], gathered, jnp.zeros_like(gathered))
    returned = lax.all_to_all(outgoing, "seq", split_axis=0, concat_axis=0, tiled=True)
    head_list = jnp.arange(HEADS)
    head_start = (head_list * total_slots + HEADS - 1) // HEADS
    sharers = ((head_list + 1) * total_slots + HEADS - 1) // HEADS - head_start
    owner_slot = head_start + ((my_index + 1) * sharers - 1) // devices
    pieces = returned[owner_slot // per_device, owner_slot % per_device]
    return pieces.transpose(1, 0, 2).reshape(TILE, HEADS * HEAD_DIM)


CHUNK = 4
ROWS = 16


def fused_kernel(
    devices,
    per_chip,
    tiles_hbm,
    count_hbm,
    q_hbm,
    k_hbm,
    qg_ref,
    kg_ref,
    v_ref,
    out_ref,
    qk_out,
    done_buf,
    score_buf,
    qk_send,
    v_send,
    o_send,
    qk_recv,
    v_recv,
    o_recv,
    loads,
    tiles_ref,
    count_ref,
    q_ref,
    k_ref,
    *landing,
):
    me = lax.axis_index("seq")
    first = (per_chip + 1) // 2
    second = per_chip - first
    qk_in, v_in = landing[:first], landing[first:]
    keep = tiles_ref.shape[1]
    scale = math.log2(math.e) / math.sqrt(HEAD_DIM)

    def slots_of(device):
        return first - lax.rem(device, 2) * (first - second)

    def head_of(device, slot):
        return (device // 2) * per_chip + lax.rem(device, 2) * first + slot

    def columns(head):
        return pl.ds(pl.multiple_of(head * HEAD_DIM, HEAD_DIM), HEAD_DIM)

    load_q = pltpu.make_async_copy(q_hbm, q_ref, loads.at[0])
    load_k = pltpu.make_async_copy(k_hbm, k_ref, loads.at[1])
    load_tiles = pltpu.make_async_copy(tiles_hbm, tiles_ref, loads.at[2])
    load_count = pltpu.make_async_copy(count_hbm, count_ref, loads.at[3])
    barrier = pltpu.get_barrier_semaphore()

    @pl.loop(1, devices)
    def _(step):
        pl.semaphore_signal(barrier, inc=1, device_id={"seq": lax.rem(me + step, devices)})

    load_q.start()
    load_k.start()
    load_tiles.start()
    load_count.start()
    pl.semaphore_wait(barrier, devices - 1)

    def v_copy(head, slot, device):
        return pltpu.make_async_remote_copy(
            src_ref=v_ref.at[:, columns(head)],
            dst_ref=v_in[slot].at[me],
            send_sem=v_send,
            recv_sem=v_recv.at[slot],
            device_id={"seq": device},
        )

    def qk_copy(head, slot, device):
        return pltpu.make_async_remote_copy(
            src_ref=qk_out.at[head],
            dst_ref=qk_in[slot].at[me],
            send_sem=qk_send,
            recv_sem=qk_recv.at[slot],
            device_id={"seq": device},
        )

    def own_v(head, slot):
        return pltpu.make_async_copy(v_ref.at[:, columns(head)], v_in[slot].at[me], v_recv.at[slot])

    def own_qk(head, slot):
        return pltpu.make_async_copy(qk_out.at[head], qk_in[slot].at[me], qk_recv.at[slot])

    half_size = devices // 2
    my_half = me // half_size

    def partner(step, same):
        half = my_half if same else 1 - my_half
        return half * half_size + lax.rem(me + step, half_size)

    def send_slot(remote, own, slot):
        @pl.loop(0, devices)
        def _(step):
            half = lax.rem(my_half + 1 + step, 2)
            device = half * half_size + lax.rem(me + step // 2, half_size)
            head = head_of(device, slot)
            there = slot < slots_of(device)

            @pl.when(jnp.logical_and(there, device != me))
            def _():
                remote(head, slot, device).start()

            @pl.when(jnp.logical_and(there, device == me))
            def _():
                own(head, slot).start()

    def send_all(remote, own):
        for slot in range(first):
            send_slot(remote, own, slot)

    send_all(v_copy, own_v)

    def norm_into(rows_ref, gain_ref, which):
        @pl.loop(0, TILE // ROWS)
        def _(block):
            rows = pl.ds(pl.multiple_of(block * ROWS, ROWS), ROWS)
            wide = rows_ref[rows, :].astype(jnp.float32)
            factor = lax.rsqrt(jnp.mean(wide * wide, axis=-1, keepdims=True) + 1e-06)
            for head in range(HEADS):
                part = slice(head * HEAD_DIM, (head + 1) * HEAD_DIM)
                qk_out[head, which, rows, :] = (wide[:, part] * factor * gain_ref[:, part]).astype(
                    jnp.bfloat16
                )

    load_q.wait()
    norm_into(q_ref, qg_ref, 0)
    load_k.wait()
    norm_into(k_ref, kg_ref, 1)
    send_all(qk_copy, own_qk)
    load_tiles.wait()
    load_count.wait()

    def o_copy(slot, tile):
        return pltpu.make_async_remote_copy(
            src_ref=done_buf.at[slot, tile],
            dst_ref=out_ref.at[:, columns(head_of(me, slot))],
            send_sem=o_send,
            recv_sem=o_recv,
            device_id={"seq": tile},
        )

    def unit(slot, tile, half):
        head = head_of(me, slot)
        query = qk_in[slot][tile, 0]
        count = count_ref[tile, head]
        entries = [tiles_ref[tile, place, head] for place in range(keep)]
        peak = None
        for start in range(0, keep, CHUNK):
            places = range(start, start + CHUNK)
            block = jnp.concatenate([qk_in[slot][entries[place], 1] for place in places], axis=0)
            scores = lax.dot_general(
                query, block, (((1,), (1,)), ((), ())), preferred_element_type=jnp.float32
            )
            for place in places:
                at = (place - start) * TILE
                bias = jnp.where(place < count, jnp.float32(0.0), jnp.float32(-jnp.inf))
                piece = scores[:, at : at + TILE] + bias
                score_buf[half, :, place * TILE : (place + 1) * TILE] = piece
                peak = piece if peak is None else jnp.maximum(peak, piece)
        peak = jnp.max(peak, axis=-1, keepdims=True)
        total = None
        mixed = None
        for start in range(0, keep, CHUNK):
            places = range(start, start + CHUNK)
            probs = []
            for place in places:
                weights = jnp.exp2(
                    (score_buf[half, :, place * TILE : (place + 1) * TILE] - peak) * scale
                )
                total = weights if total is None else total + weights
                probs.append(weights.astype(jnp.bfloat16))
            block = jnp.concatenate([v_in[slot][entries[place]] for place in places], axis=0)
            term = jnp.dot(
                jnp.concatenate(probs, axis=1), block, preferred_element_type=jnp.float32
            )
            mixed = term if mixed is None else mixed + term
        total = jnp.sum(total, axis=-1, keepdims=True)
        done_buf[slot, tile] = (mixed / total).astype(jnp.bfloat16)

    def attend_slot(slot):
        pltpu.make_async_copy(v_in[slot], v_in[slot], v_recv.at[slot]).wait()
        pltpu.make_async_copy(qk_in[slot], qk_in[slot], qk_recv.at[slot]).wait()

        @pl.loop(0, devices // 2)
        def _(pair):
            tiles = [partner(pair, False), partner(pair, True)]
            for half in range(2):
                unit(slot, tiles[half], half)
            for half in range(2):
                tile = tiles[half]

                @pl.when(tile != me)
                def _():
                    o_copy(slot, tile).start()

                @pl.when(tile == me)
                def _():
                    pltpu.make_async_copy(
                        done_buf.at[slot, tile], out_ref.at[:, columns(head_of(me, slot))], o_recv
                    ).start()

    for slot in range(first):
        pl.when(slot < slots_of(me))(functools.partial(attend_slot, slot))

    def wait_sends(mine):
        away = HEADS - mine
        pltpu.make_async_copy(
            qk_out.at[pl.ds(0, away), 0], qk_out.at[pl.ds(0, away), 0], v_send
        ).wait()
        pltpu.make_async_copy(qk_out.at[pl.ds(0, away)], qk_out.at[pl.ds(0, away)], qk_send).wait()
        sent = done_buf.at[pl.ds(0, mine), pl.ds(0, devices - 1)]
        pltpu.make_async_copy(sent, sent, o_send).wait()

    core = lax.rem(me, 2)
    pl.when(core == 0)(lambda: wait_sends(first))
    pl.when(core == 1)(lambda: wait_sends(second))
    pltpu.make_async_copy(out_ref, out_ref, o_recv).wait()


def fused(queries, keys, values, q_gain, k_gain, key_tiles, key_count):
    devices = lax.axis_size("seq")
    per_chip = HEADS // (devices // 2)
    slots = (per_chip + 1) // 2
    block = (TILE, HEAD_DIM)
    tiles = key_tiles.transpose(1, 2, 0)
    counts = key_count.transpose(1, 0)
    return pl.pallas_call(
        functools.partial(fused_kernel, devices, per_chip),
        out_shape=jax.ShapeDtypeStruct(queries.shape, jnp.bfloat16),
        in_specs=[
            pl.BlockSpec(memory_space=pl.ANY),
            pl.BlockSpec(memory_space=pl.ANY),
            pl.BlockSpec(memory_space=pl.ANY),
            pl.BlockSpec(memory_space=pl.ANY),
            pl.BlockSpec(memory_space=pltpu.VMEM),
            pl.BlockSpec(memory_space=pltpu.VMEM),
            pl.BlockSpec(memory_space=pl.ANY),
        ],
        out_specs=pl.BlockSpec(memory_space=pl.ANY),
        scratch_shapes=[
            pltpu.VMEM((HEADS, 2) + block, jnp.bfloat16),
            pltpu.VMEM((slots, devices) + block, jnp.bfloat16),
            pltpu.VMEM((2, TILE, key_tiles.shape[2] * TILE), jnp.float32),
            pltpu.SemaphoreType.DMA,
            pltpu.SemaphoreType.DMA,
            pltpu.SemaphoreType.DMA,
            pltpu.SemaphoreType.DMA((slots,)),
            pltpu.SemaphoreType.DMA((slots,)),
            pltpu.SemaphoreType.DMA,
            pltpu.SemaphoreType.DMA((4,)),
            pltpu.SMEM(tiles.shape, jnp.int32),
            pltpu.SMEM(counts.shape, jnp.int32),
            pltpu.VMEM(queries.shape, jnp.bfloat16),
            pltpu.VMEM(keys.shape, jnp.bfloat16),
        ]
        + [pltpu.VMEM((devices, 2) + block, jnp.bfloat16)] * slots
        + [pltpu.VMEM((devices,) + block, jnp.bfloat16)] * slots,
        compiler_params=pltpu.CompilerParams(
            collective_id=0, has_side_effects=True, vmem_limit_bytes=60000 * 1024
        ),
    )(
        tiles,
        counts,
        queries,
        keys,
        q_gain.reshape(1, -1),
        k_gain.reshape(1, -1),
        values,
    )


def local(queries, keys, values, q_gain, k_gain, key_tiles, key_count):
    devices = lax.axis_size("seq")
    whole_heads = devices % 2 == 0 and HEADS % (devices // 2) == 0 and 2 * HEADS >= 2 * devices
    if whole_heads and queries.shape[0] == TILE and key_tiles.shape[2] % CHUNK == 0:
        return fused(queries, keys, values, q_gain, k_gain, key_tiles, key_count)
    return exchanged(queries, keys, values, q_gain, k_gain, key_tiles, key_count)


def solution(mesh):
    in_specs = (
        P(("groups", "seq"), None),
        P(("groups", "seq"), None),
        P(("groups", "seq"), None),
        P(),
        P(),
        P(),
        P(),
    )
    out_specs = P(("groups", "seq"), None)
    return jax.shard_map(local, mesh=mesh, in_specs=in_specs, out_specs=out_specs, check_vma=False)
```

profile of v0, /device:TPU:0, one launch (start us, length us, event | category | flops | bytes accessed | tf_op | source)
XLA Modules:
  0.0 123.2 jit_solution(8145673791605512146)
XLA Ops:
  0.0 120.7 %shard_map.73 = bf16[128,5120]{1,0:T(8,128)(2,1)} custom-call(s32[16,16,40]{2,1,0:T(8,128)} %bitcast.4, s32[16,40]{1,0:T(8,128)} %bitcast.7, bf16[128,5120]{1,0:T(8,128)(2,1)} %q_hbm.1, bf16[128,5120]{1,0:T(8,128)(2,1)} %k_hbm.1, f32[1,5120]{1,0:T(1,128)} %bitcast.5, f32[1,5120]{1,0:T(1,128)} %bitcast.6, bf16[128,5120]{1,0:T(8,128)(2,1)} %v_ref.1), custom_call_target="tpu_custom_call" | custom-call | tf_op jit(solution)/shard_map/pallas_call | solution.py:353
  120.7 2.5 %copy.9 = bf16[128,5120]{1,0:T(8,128)(2,1)} copy(bf16[128,5120]{1,0:T(8,128)(2,1)} %shard_map.73) | data formatting | bytes 2621440
where the time goes:
time: 123 us
  Pallas kernels  121 us (98%)
  local copies, waits for them, and re-layouts  2.46 us (2%)
    pallas_call x1, Pallas kernels, fused(): pl.pallas_call(functools.partial(fused_kernel, devices, per_chip), out_sh...  121 us

commit v1 on v0

--- a/solution.py
+++ b/solution.py
@@ -131,8 +131,8 @@
     count_hbm,
     q_hbm,
     k_hbm,
-    qg_ref,
-    kg_ref,
+    qg_hbm,
+    kg_hbm,
     v_ref,
     out_ref,
     qk_out,
@@ -149,6 +149,8 @@
     count_ref,
     q_ref,
     k_ref,
+    qg_ref,
+    kg_ref,
     *landing,
 ):
     me = lax.axis_index("seq")
@@ -171,12 +173,16 @@
     load_k = pltpu.make_async_copy(k_hbm, k_ref, loads.at[1])
     load_tiles = pltpu.make_async_copy(tiles_hbm, tiles_ref, loads.at[2])
     load_count = pltpu.make_async_copy(count_hbm, count_ref, loads.at[3])
+    load_qg = pltpu.make_async_copy(qg_hbm, qg_ref, loads.at[4])
+    load_kg = pltpu.make_async_copy(kg_hbm, kg_ref, loads.at[5])
     barrier = pltpu.get_barrier_semaphore()
 
     @pl.loop(1, devices)
     def _(step):
         pl.semaphore_signal(barrier, inc=1, device_id={"seq": lax.rem(me + step, devices)})
 
+    load_qg.start()
+    load_kg.start()
     load_q.start()
     load_k.start()
     load_tiles.start()
@@ -209,10 +215,6 @@
 
     half_size = devices // 2
     my_half = me // half_size
-
-    def partner(step, same):
-        half = my_half if same else 1 - my_half
-        return half * half_size + lax.rem(me + step, half_size)
 
     def send_slot(remote, own, slot):
         @pl.loop(0, devices)
@@ -248,6 +250,8 @@
                     jnp.bfloat16
                 )
 
+    load_qg.wait()
+    load_kg.wait()
     load_q.wait()
     norm_into(q_ref, qg_ref, 0)
     load_k.wait()
@@ -309,7 +313,9 @@
 
         @pl.loop(0, devices // 2)
         def _(pair):
-            tiles = [partner(pair, False), partner(pair, True)]
+            quarter = devices // 4
+            order = pair // quarter * quarter + lax.rem(me + pair, quarter)
+            tiles = [(1 - my_half) * half_size + order, my_half * half_size + order]
             for half in range(2):
                 unit(slot, tiles[half], half)
             for half in range(2):
@@ -353,15 +359,7 @@
     return pl.pallas_call(
         functools.partial(fused_kernel, devices, per_chip),
         out_shape=jax.ShapeDtypeStruct(queries.shape, jnp.bfloat16),
-        in_specs=[
-            pl.BlockSpec(memory_space=pl.ANY),
-            pl.BlockSpec(memory_space=pl.ANY),
-            pl.BlockSpec(memory_space=pl.ANY),
-            pl.BlockSpec(memory_space=pl.ANY),
-            pl.BlockSpec(memory_space=pltpu.VMEM),
-            pl.BlockSpec(memory_space=pltpu.VMEM),
-            pl.BlockSpec(memory_space=pl.ANY),
-        ],
+        in_specs=[pl.BlockSpec(memory_space=pl.ANY)] * 7,
         out_specs=pl.BlockSpec(memory_space=pl.ANY),
         scratch_shapes=[
             pltpu.VMEM((HEADS, 2) + block, jnp.bfloat16),
@@ -373,25 +371,32 @@
             pltpu.SemaphoreType.DMA((slots,)),
             pltpu.SemaphoreType.DMA((slots,)),
             pltpu.SemaphoreType.DMA,
-            pltpu.SemaphoreType.DMA((4,)),
+            pltpu.SemaphoreType.DMA((6,)),
             pltpu.SMEM(tiles.shape, jnp.int32),
             pltpu.SMEM(counts.shape, jnp.int32),
             pltpu.VMEM(queries.shape, jnp.bfloat16),
             pltpu.VMEM(keys.shape, jnp.bfloat16),
+            pltpu.VMEM((1, q_gain.shape[0]), jnp.float32),
+            pltpu.VMEM((1, k_gain.shape[0]), jnp.float32),
         ]
         + [pltpu.VMEM((devices, 2) + block, jnp.bfloat16)] * slots
         + [pltpu.VMEM((devices,) + block, jnp.bfloat16)] * slots,
         compiler_params=pltpu.CompilerParams(
-            collective_id=0, has_side_effects=True, vmem_limit_bytes=60000 * 1024
+            collective_id=0, has_side_effects=True, vmem_limit_bytes=24000 * 1024
         ),
     )(
-        tiles,
-        counts,
-        queries,
-        keys,
-        q_gain.reshape(1, -1),
-        k_gain.reshape(1, -1),
-        values,
+        *[
+            pltpu.with_memory_space_constraint(array, pltpu.HBM)
+            for array in (
+                tiles,
+                counts,
+                queries,
+                keys,
+                q_gain.reshape(1, -1),
+                k_gain.reshape(1, -1),
+                values,
+            )
+        ]
     )
 
 

time: 123 us -> 120 us (0.976)
  Pallas kernels: 121 us -> 119 us
  local copies, waits for them, and re-layouts: 2.46 us -> 1.06 us
    pallas_call x1, Pallas kernels: 121 us -> 119 us  [fused(): pl.pallas_call(functools.partial(fused_kernel, devices, per_chip), out_sh...]
    unnamed x1, local copies, waits for them, and re-layouts: 2.46 us -> 1.06 us
where the time goes in v1:
time: 120 us
  Pallas kernels  119 us (99%)
    pallas_call x1, Pallas kernels, fused(): pl.pallas_call(functools.partial(fused_kernel, devices, per_chip), out_sh...  119 us

profile of v1, /device:TPU:0, one launch (start us, length us, event | category | flops | bytes accessed | tf_op | source)
XLA Modules:
  0.0 119.8 jit_solution(12832997472160051451)
XLA Ops:
  0.0 118.7 %shard_map.73 = bf16[128,5120]{1,0:T(8,128)(2,1)S(1)} custom-call(s32[16,16,40]{2,1,0:T(8,128)} %bitcast.4, s32[16,40]{1,0:T(8,128)} %bitcast.7, bf16[128,5120]{1,0:T(8,128)(2,1)} %q_hbm.1, bf16[128,5120]{1,0:T(8,128)(2,1)} %k_hbm.1, f32[1,5120]{1,0:T(1,128)} %bitcast.5, f32[1,5120]{1,0:T(1,128)} %bitcast.6, bf16[128,5120]{1,0:T(8,128)(2,1)} %v_ref.1), custom_call_target="tpu_custom_call" | custom-call | tf_op jit(solution)/shard_map/pallas_call | solution.py:359
  118.7 1.1 copy.9

commit v2 on v1

--- a/solution.py
+++ b/solution.py
@@ -145,6 +145,8 @@
     v_recv,
     o_recv,
     loads,
+    outer_in,
+    all_in,
     tiles_ref,
     count_ref,
     q_ref,
@@ -176,10 +178,16 @@
     load_qg = pltpu.make_async_copy(qg_hbm, qg_ref, loads.at[4])
     load_kg = pltpu.make_async_copy(kg_hbm, kg_ref, loads.at[5])
     barrier = pltpu.get_barrier_semaphore()
-
-    @pl.loop(1, devices)
-    def _(step):
-        pl.semaphore_signal(barrier, inc=1, device_id={"seq": lax.rem(me + step, devices)})
+    half_size = devices // 2
+    quarter = devices // 4
+    my_half = me // half_size
+    middle = jnp.logical_and(me >= quarter, me < devices - quarter)
+
+    @pl.when(middle)
+    def _():
+        @pl.loop(1, devices)
+        def _(step):
+            pl.semaphore_signal(barrier, inc=1, device_id={"seq": lax.rem(me + step, devices)})
 
     load_qg.start()
     load_kg.start()
@@ -187,7 +195,16 @@
     load_k.start()
     load_tiles.start()
     load_count.start()
-    pl.semaphore_wait(barrier, devices - 1)
+    pl.semaphore_wait(barrier, half_size - middle.astype(jnp.int32))
+
+    @pl.when(jnp.logical_not(middle))
+    def _():
+        @pl.loop(0, half_size)
+        def _(step):
+            pl.semaphore_signal(
+                outer_in, inc=1, device_id={"seq": quarter + lax.rem(me + step, half_size)}
+            )
+
 
     def v_copy(head, slot, device):
         return pltpu.make_async_remote_copy(
@@ -213,14 +230,11 @@
     def own_qk(head, slot):
         return pltpu.make_async_copy(qk_out.at[head], qk_in[slot].at[me], qk_recv.at[slot])
 
-    half_size = devices // 2
-    my_half = me // half_size
-
-    def send_slot(remote, own, slot):
-        @pl.loop(0, devices)
+    def send_slot(remote, own, slot, device_at, steps):
+        @pl.loop(0, steps)
         def _(step):
             half = lax.rem(my_half + 1 + step, 2)
-            device = half * half_size + lax.rem(me + step // 2, half_size)
+            device = device_at(half, step // 2)
             head = head_of(device, slot)
             there = slot < slots_of(device)
 
@@ -232,11 +246,33 @@
             def _():
                 own(head, slot).start()
 
-    def send_all(remote, own):
+    def any_device(half, step):
+        return half * half_size + lax.rem(me + step, half_size)
+
+    def middle_device(half, step):
+        return quarter + half * quarter + lax.rem(me + step, quarter)
+
+    def outer_device(half, step):
+        return half * (devices - quarter) + lax.rem(me + step, quarter)
+
+    def send_all(remote, own, device_at, steps):
         for slot in range(first):
-            send_slot(remote, own, slot)
-
-    send_all(v_copy, own_v)
+            send_slot(remote, own, slot, device_at, steps)
+
+    send_all(v_copy, own_v, middle_device, half_size)
+
+    @pl.when(middle)
+    def _():
+        pl.semaphore_wait(outer_in, half_size)
+        pl.semaphore_signal(
+            all_in, inc=1, device_id={"seq": me + (2 * my_half - 1) * quarter}
+        )
+
+    @pl.when(jnp.logical_not(middle))
+    def _():
+        pl.semaphore_wait(all_in, 1)
+
+    send_all(v_copy, own_v, outer_device, half_size)
 
     def norm_into(rows_ref, gain_ref, which):
         @pl.loop(0, TILE // ROWS)
@@ -256,7 +292,7 @@
     norm_into(q_ref, qg_ref, 0)
     load_k.wait()
     norm_into(k_ref, kg_ref, 1)
-    send_all(qk_copy, own_qk)
+    send_all(qk_copy, own_qk, any_device, devices)
     load_tiles.wait()
     load_count.wait()
 
@@ -313,7 +349,6 @@
 
         @pl.loop(0, devices // 2)
         def _(pair):
-            quarter = devices // 4
             order = pair // quarter * quarter + lax.rem(me + pair, quarter)
             tiles = [(1 - my_half) * half_size + order, my_half * half_size + order]
             for half in range(2):
@@ -372,6 +407,8 @@
             pltpu.SemaphoreType.DMA((slots,)),
             pltpu.SemaphoreType.DMA,
             pltpu.SemaphoreType.DMA((6,)),
+            pltpu.SemaphoreType.REGULAR,
+            pltpu.SemaphoreType.REGULAR,
             pltpu.SMEM(tiles.shape, jnp.int32),
             pltpu.SMEM(counts.shape, jnp.int32),
             pltpu.VMEM(queries.shape, jnp.bfloat16),
@@ -402,7 +439,7 @@
 
 def local(queries, keys, values, q_gain, k_gain, key_tiles, key_count):
     devices = lax.axis_size("seq")
-    whole_heads = devices % 2 == 0 and HEADS % (devices // 2) == 0 and 2 * HEADS >= 2 * devices
+    whole_heads = devices % 4 == 0 and HEADS % (devices // 2) == 0 and 2 * HEADS >= 2 * devices
     if whole_heads and queries.shape[0] == TILE and key_tiles.shape[2] % CHUNK == 0:
         return fused(queries, keys, values, q_gain, k_gain, key_tiles, key_count)
     return exchanged(queries, keys, values, q_gain, k_gain, key_tiles, key_count)

time: 120 us -> 119 us (level)
  Pallas kernels: 119 us -> 117 us
    pallas_call x1, Pallas kernels: 119 us -> 117 us  [fused(): pl.pallas_call(functools.partial(fused_kernel, devices, per_chip), out_sh...]
where the time goes in v2:
time: 119 us; the launch traced here: 118 us
  Pallas kernels  117 us (98%)
    pallas_call x1, Pallas kernels, fused(): pl.pallas_call(functools.partial(fused_kernel, devices, per_chip), out_sh...  117 us

profile of v2, /device:TPU:0, one launch (start us, length us, event | category | flops | bytes accessed | tf_op | source)
XLA Modules:
  0.0 118.5 jit_solution(16032469792751623881)
XLA Ops:
  0.0 117.4 %shard_map.73 = bf16[128,5120]{1,0:T(8,128)(2,1)S(1)} custom-call(s32[16,16,40]{2,1,0:T(8,128)} %bitcast.4, s32[16,40]{1,0:T(8,128)} %bitcast.7, bf16[128,5120]{1,0:T(8,128)(2,1)} %q_hbm.1, bf16[128,5120]{1,0:T(8,128)(2,1)} %k_hbm.1, f32[1,5120]{1,0:T(1,128)} %bitcast.5, f32[1,5120]{1,0:T(1,128)} %bitcast.6, bf16[128,5120]{1,0:T(8,128)(2,1)} %v_ref.1), custom_call_target="tpu_custom_call" | custom-call | tf_op jit(solution)/shard_map/pallas_call | solution.py:394
  117.4 1.1 copy.9

commit v3 on v2

--- a/solution.py
+++ b/solution.py
@@ -182,12 +182,28 @@
     quarter = devices // 4
     my_half = me // half_size
     middle = jnp.logical_and(me >= quarter, me < devices - quarter)
+    chip = lax.rem(me, quarter) // 2 * 2
+
+    def near_device(half, step):
+        return quarter + half * quarter + chip + lax.rem(me + step, 2)
+
+    def outer_device(half, step):
+        return half * (devices - quarter) + lax.rem(me + step, quarter)
 
     @pl.when(middle)
     def _():
-        @pl.loop(1, devices)
+        @pl.loop(0, 4)
         def _(step):
-            pl.semaphore_signal(barrier, inc=1, device_id={"seq": lax.rem(me + step, devices)})
+            device = near_device(lax.rem(my_half + 1 + step, 2), step // 2)
+
+            @pl.when(device != me)
+            def _():
+                pl.semaphore_signal(barrier, inc=1, device_id={"seq": device})
+
+        @pl.loop(0, half_size)
+        def _(step):
+            device = outer_device(lax.rem(my_half + 1 + step, 2), step // 2)
+            pl.semaphore_signal(barrier, inc=1, device_id={"seq": device})
 
     load_qg.start()
     load_kg.start()
@@ -195,7 +211,7 @@
     load_k.start()
     load_tiles.start()
     load_count.start()
-    pl.semaphore_wait(barrier, half_size - middle.astype(jnp.int32))
+    pl.semaphore_wait(barrier, jnp.where(middle, 3, half_size))
 
     @pl.when(jnp.logical_not(middle))
     def _():
@@ -204,7 +220,6 @@
             pl.semaphore_signal(
                 outer_in, inc=1, device_id={"seq": quarter + lax.rem(me + step, half_size)}
             )
-
 
     def v_copy(head, slot, device):
         return pltpu.make_async_remote_copy(
@@ -249,27 +264,29 @@
     def any_device(half, step):
         return half * half_size + lax.rem(me + step, half_size)
 
+    def far_device(half, step):
+        place = lax.rem(chip + 2 + step // 2 * 2 + lax.rem(me + step, 2), quarter)
+        return quarter + half * quarter + place
+
     def middle_device(half, step):
         return quarter + half * quarter + lax.rem(me + step, quarter)
-
-    def outer_device(half, step):
-        return half * (devices - quarter) + lax.rem(me + step, quarter)
 
     def send_all(remote, own, device_at, steps):
         for slot in range(first):
             send_slot(remote, own, slot, device_at, steps)
 
-    send_all(v_copy, own_v, middle_device, half_size)
-
     @pl.when(middle)
     def _():
+        send_all(v_copy, own_v, near_device, 4)
         pl.semaphore_wait(outer_in, half_size)
         pl.semaphore_signal(
             all_in, inc=1, device_id={"seq": me + (2 * my_half - 1) * quarter}
         )
+        send_all(v_copy, own_v, far_device, half_size - 4)
 
     @pl.when(jnp.logical_not(middle))
     def _():
+        send_all(v_copy, own_v, middle_device, half_size)
         pl.semaphore_wait(all_in, 1)
 
     send_all(v_copy, own_v, outer_device, half_size)
@@ -349,7 +366,7 @@
 
         @pl.loop(0, devices // 2)
         def _(pair):
-            order = pair // quarter * quarter + lax.rem(me + pair, quarter)
+            order = pair // 2 * 2 + lax.rem(me + pair, 2)
             tiles = [(1 - my_half) * half_size + order, my_half * half_size + order]
             for half in range(2):
                 unit(slot, tiles[half], half)
@@ -439,7 +456,7 @@
 
 def local(queries, keys, values, q_gain, k_gain, key_tiles, key_count):
     devices = lax.axis_size("seq")
-    whole_heads = devices % 4 == 0 and HEADS % (devices // 2) == 0 and 2 * HEADS >= 2 * devices
+    whole_heads = devices % 8 == 0 and HEADS % (devices // 2) == 0 and 2 * HEADS >= 2 * devices
     if whole_heads and queries.shape[0] == TILE and key_tiles.shape[2] % CHUNK == 0:
         return fused(queries, keys, values, q_gain, k_gain, key_tiles, key_count)
     return exchanged(queries, keys, values, q_gain, k_gain, key_tiles, key_count)

time: 119 us -> 118 us (level)
  no operation moved by 1% of the time
where the time goes in v3:
time: 118 us; the launch traced here: 117 us
  Pallas kernels  116 us (98%)
    pallas_call x1, Pallas kernels, fused(): pl.pallas_call(functools.partial(fused_kernel, devices, per_chip), out_sh...  116 us

profile of v3, /device:TPU:0, one launch (start us, length us, event | category | flops | bytes accessed | tf_op | source)
XLA Modules:
  0.0 117.4 jit_solution(6214550767543094959)
XLA Ops:
  0.0 116.3 %shard_map.73 = bf16[128,5120]{1,0:T(8,128)(2,1)S(1)} custom-call(s32[16,16,40]{2,1,0:T(8,128)} %bitcast.4, s32[16,40]{1,0:T(8,128)} %bitcast.7, bf16[128,5120]{1,0:T(8,128)(2,1)} %q_hbm.1, bf16[128,5120]{1,0:T(8,128)(2,1)} %k_hbm.1, f32[1,5120]{1,0:T(1,128)} %bitcast.5, f32[1,5120]{1,0:T(1,128)} %bitcast.6, bf16[128,5120]{1,0:T(8,128)(2,1)} %v_ref.1), custom_call_target="tpu_custom_call" | custom-call | tf_op jit(solution)/shard_map/pallas_call | solution.py:411
  116.3 1.1 copy.9

commit v4 on v3

--- a/solution.py
+++ b/solution.py
@@ -360,28 +360,46 @@
         total = jnp.sum(total, axis=-1, keepdims=True)
         done_buf[slot, tile] = (mixed / total).astype(jnp.bfloat16)
 
+    def tiles_at(pair):
+        core = 1 - lax.rem(pair, 2)
+        return [
+            half * half_size + lax.rem(pair // 2 * 2 + half * quarter, half_size) + core
+            for half in (1 - my_half, my_half)
+        ]
+
+    def return_tiles(slot, pair):
+        for tile in tiles_at(pair):
+
+            @pl.when(tile != me)
+            def _():
+                o_copy(slot, tile).start()
+
+            @pl.when(tile == me)
+            def _():
+                pltpu.make_async_copy(
+                    done_buf.at[slot, tile], out_ref.at[:, columns(head_of(me, slot))], o_recv
+                ).start()
+
     def attend_slot(slot):
         pltpu.make_async_copy(v_in[slot], v_in[slot], v_recv.at[slot]).wait()
         pltpu.make_async_copy(qk_in[slot], qk_in[slot], qk_recv.at[slot]).wait()
+        last = slots_of(me) - 1
 
         @pl.loop(0, devices // 2)
         def _(pair):
-            order = pair // 2 * 2 + lax.rem(me + pair, 2)
-            tiles = [(1 - my_half) * half_size + order, my_half * half_size + order]
+            tiles = tiles_at(pair)
             for half in range(2):
                 unit(slot, tiles[half], half)
-            for half in range(2):
-                tile = tiles[half]
-
-                @pl.when(tile != me)
+            late = pair >= quarter
+            if slot > 0:
+
+                @pl.when(jnp.logical_and(late, slot == last))
                 def _():
-                    o_copy(slot, tile).start()
-
-                @pl.when(tile == me)
-                def _():
-                    pltpu.make_async_copy(
-                        done_buf.at[slot, tile], out_ref.at[:, columns(head_of(me, slot))], o_recv
-                    ).start()
+                    return_tiles(slot - 1, pair)
+
+            @pl.when(jnp.logical_not(jnp.logical_and(late, slot == last - 1)))
+            def _():
+                return_tiles(slot, pair)
 
     for slot in range(first):
         pl.when(slot < slots_of(me))(functools.partial(attend_slot, slot))

time: 118 us -> 118 us (level); the launches traced: 117 us -> 116 us
    pallas_call x1, Pallas kernels: 116 us -> 115 us  [fused(): pl.pallas_call(functools.partial(fused_kernel, devices, per_chip), out_sh...]
where the time goes in v4:
time: 118 us; the launch traced here: 116 us
  Pallas kernels  115 us (97%)
    pallas_call x1, Pallas kernels, fused(): pl.pallas_call(functools.partial(fused_kernel, devices, per_chip), out_sh...  115 us

profile of v4, /device:TPU:0, one launch (start us, length us, event | category | flops | bytes accessed | tf_op | source)
XLA Modules:
  0.0 116.1 jit_solution(11309587507255193622)
XLA Ops:
  0.0 115.0 %shard_map.73 = bf16[128,5120]{1,0:T(8,128)(2,1)S(1)} custom-call(s32[16,16,40]{2,1,0:T(8,128)} %bitcast.4, s32[16,40]{1,0:T(8,128)} %bitcast.7, bf16[128,5120]{1,0:T(8,128)(2,1)} %q_hbm.1, bf16[128,5120]{1,0:T(8,128)(2,1)} %k_hbm.1, f32[1,5120]{1,0:T(1,128)} %bitcast.5, f32[1,5120]{1,0:T(1,128)} %bitcast.6, bf16[128,5120]{1,0:T(8,128)(2,1)} %v_ref.1), custom_call_target="tpu_custom_call" | custom-call | tf_op jit(solution)/shard_map/pallas_call | solution.py:429
  115.0 1.1 copy.9
